TPU v7x, 32 devices: a whole 2x2x4 slice. The times are simulated.
32 devices in a mesh: rx: 4 (over y, x), chirp: 8 (over z, core).
Axes of the slice: x: 2, y: 2, z: 4, core: 2. Of those that a mesh axis runs over, the one named last changes fastest.
Arguments:
- samples: bfloat16 [2, 128, 128, 4096], P(None, None, 'rx', 'chirp'), may hold values from -6 to 6
- tx_offsets: int32 [12], replicated, may hold values from 0 to 3840, as said below
- band_owner: int32 [16], replicated, may hold values from 0 to 3, as said below
- beam_weights: bfloat16 [2, 256, 1536], replicated, may hold values from -0.109375 to 0.109375
Outputs:
- tile_store: bfloat16 [48, 2, 256, 2048], P('rx', None, None, 'chirp')
Inputs may be any that keep to these rules, and one draw needn't show every extreme that they name: `tx_offsets`: each offset is 256 times a Doppler slot of 0 to 15; transmitters use different slots, and slots 0 and 15 are always used. `band_owner`: at most 12 bands share an owner, and one owner has exactly 12.
All inputs are finite; a program needn't handle non-finite values.
Results may differ from a plain program's by a relative error of at most 0.007.
Values may be sent and summed in bfloat16 or wider, within the bound.
No kernel may reach another device: no remote copies, remote signals or barrier semaphores. Data moves between devices by JAX's collectives and lax.ppermute only.
A program may use at most 192 MiB of HBM per device.

v0:
```python
from functools import partial
import math

import jax
import jax.numpy as jnp
from jax import lax
from jax.sharding import PartitionSpec as P

K1 = 64
K2 = 64
SLOTS = 16


def dft_pair(size):
    indices = jnp.arange(size, dtype=jnp.int32)
    product = indices[:, None] * indices[None, :] % size
    phase_angle = product.astype(jnp.float32) * (-2.0 * math.pi / size)
    scale = 1.0 / math.sqrt(size)
    return (
        (jnp.cos(phase_angle) * scale).astype(jnp.bfloat16),
        (jnp.sin(phase_angle) * scale).astype(jnp.bfloat16),
    )


def twiddle_table():
    outer = jnp.arange(K1, dtype=jnp.int32)[:, None]
    inner = jnp.arange(K2, dtype=jnp.int32)[None, :]
    phase_angle = (outer * inner % (K1 * K2)).astype(jnp.float32) * (-2.0 * math.pi / (K1 * K2))
    return (jnp.cos(phase_angle), jnp.sin(phase_angle))


def spectrum_of(real_part, imag_part, row_count):
    mixing = partial(jnp.einsum, preferred_element_type=jnp.float32)
    split_re = real_part.reshape(row_count, K1, K2)
    split_im = imag_part.reshape(row_count, K1, K2)
    table_re, table_im = dft_pair(K1)
    section_re = mixing("kn,rnm->rkm", table_re, split_re) - mixing(
        "kn,rnm->rkm", table_im, split_im
    )
    section_im = mixing("kn,rnm->rkm", table_re, split_im) + mixing(
        "kn,rnm->rkm", table_im, split_re
    )
    twist_re, twist_im = twiddle_table()
    turned_re = (section_re * twist_re - section_im * twist_im).astype(jnp.bfloat16)
    turned_im = (section_re * twist_im + section_im * twist_re).astype(jnp.bfloat16)
    final_re, final_im = dft_pair(K2)
    out_re = mixing("qm,rkm->rqk", final_re, turned_re) - mixing("qm,rkm->rqk", final_im, turned_im)
    out_im = mixing("qm,rkm->rqk", final_re, turned_im) + mixing("qm,rkm->rqk", final_im, turned_re)
    return (
        out_re.reshape(row_count, K1 * K2).astype(jnp.bfloat16),
        out_im.reshape(row_count, K1 * K2).astype(jnp.bfloat16),
    )


def shards(samples, tx_offsets, band_owner, beam_weights):
    owners = lax.axis_size("rx")
    band_count = band_owner.shape[0]
    capacity = 3 * band_count // owners
    tx_count = tx_offsets.shape[0]
    bin_count = K1 * K2
    speed_bins = bin_count // SLOTS
    band_width = speed_bins // band_count
    starts = (tx_offsets - speed_bins // 2) % bin_count
    sender = jnp.arange(tx_count, dtype=jnp.int32)[:, None]
    speed = jnp.arange(speed_bins, dtype=jnp.int32)[None, :] - speed_bins // 2
    phase_angle = (sender * speed).astype(jnp.float32) * (-2.0 * math.pi / (tx_count * speed_bins))
    cos_part = jnp.cos(phase_angle)[:, None, None, :]
    sin_part = jnp.sin(phase_angle)[:, None, None, :]
    pieces = lax.all_to_all(samples, "chirp", split_axis=1, concat_axis=3, tiled=True)
    bin_rows = pieces.shape[1]
    item_count = pieces.shape[2]
    spec_re, spec_im = spectrum_of(
        pieces[0].reshape(bin_rows * item_count, bin_count),
        pieces[1].reshape(bin_rows * item_count, bin_count),
        bin_rows * item_count,
    )
    joined = jnp.stack([spec_re, spec_im]).reshape(2, bin_rows, item_count, bin_count)
    double = jnp.concatenate([joined, joined], axis=3)

    def take_band(begin_at):
        return lax.dynamic_slice_in_dim(double, begin_at, speed_bins, 3)

    picked = jax.vmap(take_band)(starts)
    got_re = picked[:, 0].astype(jnp.float32)
    got_im = picked[:, 1].astype(jnp.float32)
    demux_re = got_re * cos_part - got_im * sin_part
    demux_im = got_re * sin_part + got_im * cos_part
    demuxed = jnp.stack([demux_re, demux_im]).astype(jnp.bfloat16)
    demuxed = demuxed.transpose(0, 1, 3, 2, 4)
    rx_local = demuxed.shape[2]
    bin_rows = demuxed.shape[3]
    tile_width = bin_rows * band_width
    tiles = demuxed.reshape(2, tx_count, rx_local, bin_rows, band_count, band_width)
    tiles = tiles.transpose(4, 0, 1, 2, 3, 5).reshape(band_count, 2, tx_count, rx_local, tile_width)
    counter = jnp.arange(band_count, dtype=jnp.int32)
    same_owner = band_owner[:, None] == band_owner[None, :]
    earlier = counter[None, :] < counter[:, None]
    band_rank = jnp.sum((same_owner & earlier).astype(jnp.int32), axis=1)
    weight_re = beam_weights[0]
    weight_im = beam_weights[1]
    slot_ids = band_owner * capacity + band_rank
    choose = (slot_ids[None, :] == jnp.arange(owners * capacity, dtype=jnp.int32)[:, None]).astype(
        jnp.bfloat16
    )
    outgoing = jnp.dot(
        choose, tiles.reshape(band_count, -1), preferred_element_type=jnp.float32
    ).astype(jnp.bfloat16)
    outgoing = outgoing.reshape(owners, capacity, 2, tx_count, rx_local, tile_width)
    slots = lax.all_to_all(outgoing, "rx", split_axis=0, concat_axis=4, tiled=True)[0]
    item_count = slots.shape[0]
    channels = slots.reshape(item_count, 2, slots.shape[2] * slots.shape[3], slots.shape[4])
    mixing = partial(jnp.einsum, preferred_element_type=jnp.float32)
    beam_re = mixing("bc,scm->sbm", weight_re, channels[:, 0]) - mixing(
        "bc,scm->sbm", weight_im, channels[:, 1]
    )
    beam_im = mixing("bc,scm->sbm", weight_re, channels[:, 1]) + mixing(
        "bc,scm->sbm", weight_im, channels[:, 0]
    )
    return jnp.stack([beam_re, beam_im], axis=1).astype(jnp.bfloat16)


def solution(mesh):
    placed = (P(None, None, "rx", "chirp"), P(), P(), P())
    return jax.shard_map(
        shards, mesh=mesh, in_specs=placed, out_specs=P("rx", None, None, "chirp"), check_vma=False
    )
```

profile of v0, /device:TPU:0, one launch (start us, length us, event | category | flops | bytes accessed | tf_op | source)
XLA Modules:
  0.0 832.4 jit_solution(5319038525160731027)
XLA Ops:
  0.0 8.3 copy.56
  8.3 6.5 all-to-all-start
  15.7 183.0 %all-to-all-done = bf16[2,128,32,512]{3,2,0,1:T(8,128)(2,1)} async-done(((bf16[2,128,32,512]{3,2,0,1:T(8,128)(2,1)}), bf16[2,128,32,512]{3,2,0,1:T(8,128)(2,1)}, u32[]{:S(2)}, u32[]{:S(2)}) %all-to-all-start) | async-done | bytes 8388640 | tf_op jit(solution)/shard_map/all_to_all | solution.py:69
  198.7 15.4 %copy.96 = bf16[2,8,16,32,512]{4,1,3,2,0:T(8,128)(2,1)} copy(bf16[2,8,16,32,512]{4,3,0,2,1:T(8,128)(2,1)} %bitcast.1) | data formatting | bytes 16777216 | tf_op jit(solution)/shard_map/all_to_all | solution.py:69
  214.1 5.9 fusion.107
  220.0 11.2 %reshape_reshape_squeeze.7 = bf16[512,64,64]{2,1,0:T(8,128)(2,1)} reshape(bf16[1,16,32,8,512]{4,3,2,1,0:T(8,128)(2,1)} %get-tuple-element.24) | data formatting | bytes 8388608 | tf_op jit(solution)/shard_map/reshape;reshape;squeeze | solution.py:35
  231.2 12.2 %copy.59 = bf16[512,64,64]{0,1,2:T(8,128)(2,1)} copy(bf16[512,64,64]{2,1,0:T(8,128)(2,1)} %reshape_reshape_squeeze.7) | data formatting | bytes 8388608 | tf_op jit(solution)/shard_map/reshape;reshape;squeeze | solution.py:35
  243.4 6.9 fusion.55
  250.3 4.6 fusion.59
  254.9 11.2 %reshape_reshape_squeeze.6 = bf16[512,64,64]{2,1,0:T(8,128)(2,1)} reshape(bf16[1,16,32,8,512]{4,3,2,1,0:T(8,128)(2,1)} %get-tuple-element.23) | data formatting | bytes 8388608 | tf_op jit(solution)/shard_map/reshape;reshape;squeeze | solution.py:34
  266.1 12.0 %copy.58 = bf16[512,64,64]{0,1,2:T(8,128)(2,1)} copy(bf16[512,64,64]{2,1,0:T(8,128)(2,1)} %reshape_reshape_squeeze.6) | data formatting | bytes 8388608 | tf_op jit(solution)/shard_map/reshape;reshape;squeeze | solution.py:34
  278.1 6.9 fusion.53
  285.0 12.6 %fusion.8 = (bf16[512,64,64]{0,1,2:T(8,128)(2,1)}, bf16[512,64,64]{0,1,2:T(8,128)(2,1)S(1)}) fusion(f32[64,64]{0,1:T(8,128)S(1)} %copy.63, f32[64,64]{0,1:T(8,128)S(1)} %copy.60, f32[64,512,64]{1,0,2:T(8,128)} %fusion.59, f32[64,512,64]{1,0,2:T(8,128)} %fusion.53, f32[64,512,64]{1,0,2:T(8,128)} %fusion.55, bf16[512,64,64]{0,1,2:T(8,128)(2,1)S(1)} %copy-done), kind=kOutput, calls=%fused_computation.24 | convolution fusion | flops 289472512 | bytes 37781504 | tf_op jit(solution)/shard_map/kn,rnm->rkm/dot_general | solution.py:37
  297.6 5.6 fusion.12
  303.2 8.8 %fusion.14 = f32[512,64,64]{0,2,1:T(8,128)} fusion(bf16[512,64,64]{0,1,2:T(8,128)(2,1)S(1)} %get-tuple-element.22), kind=kOutput, calls=%fused_computation.30 | convolution fusion | flops 268500992 | bytes 12582912 | tf_op jit(solution)/shard_map/qm,rkm->rqk/dot_general | solution.py:48
  312.0 7.8 fusion.10
  319.8 15.6 %copy.66 = bf16[512,64,64]{2,1,0:T(8,128)(2,1)} copy(bf16[512,64,64]{0,1,2:T(8,128)(2,1)} %fusion.10) | data formatting | bytes 8388608 | tf_op jit(solution)/shard_map/convert_element_type | solution.py:50
  335.5 12.0 %convert_element_type.170 = bf16[1,16,32,4096]{3,2,1,0:T(8,128)(2,1)} reshape(bf16[512,64,64]{2,1,0:T(8,128)(2,1)} %copy.66) | data formatting | bytes 8388608 | tf_op jit(solution)/shard_map/convert_element_type | solution.py:50
  347.5 12.4 %fusion.11 = bf16[512,64,64]{0,1,2:T(8,128)(2,1)} fusion(f32[512,64,64]{0,2,1:T(8,128)} %fusion.14, bf16[512,64,64]{0,1,2:T(8,128)(2,1)} %get-tuple-element.21), kind=kOutput, calls=%fused_computation.27 | convolution fusion | flops 272695296 | bytes 16777216 | tf_op jit(solution)/shard_map/qm,rkm->rqk/dot_general | solution.py:48
  359.9 16.1 %copy.69 = bf16[512,64,64]{2,1,0:T(8,128)(2,1)} copy(bf16[512,64,64]{0,1,2:T(8,128)(2,1)} %fusion.11) | data formatting | bytes 8388608 | tf_op jit(solution)/shard_map/convert_element_type | solution.py:51
  375.9 12.1 %convert_element_type.173 = bf16[1,16,32,4096]{3,2,1,0:T(8,128)(2,1)} reshape(bf16[512,64,64]{2,1,0:T(8,128)(2,1)} %copy.69) | data formatting | bytes 8388608 | tf_op jit(solution)/shard_map/convert_element_type | solution.py:51
  388.0 14.0 %maximum_maximum_fusion = bf16[2,16,32,8192]{3,2,1,0:T(8,128)(2,1)} fusion(bf16[1,16,32,4096]{3,2,1,0:T(8,128)(2,1)} %convert_element_type.173, bf16[1,16,32,4096]{3,2,1,0:T(8,128)(2,1)} %convert_element_type.170), kind=kLoop, calls=%fused_computation.3 | loop fusion | flops 67108864 | bytes 25165824 | tf_op jit(solution)/shard_map/concatenate | solution.py:78
  402.0 41.0 %while.1 = (s32[]{:T(128)}, bf16[2,16,32,8192]{3,2,1,0:T(8,128)(2,1)}, s32[12,4]{0,1:T(4,128)S(1)}, bf16[12,2,16,32,256]{4,3,2,0,1:T(8,128)(2,1)}, s32[]{:T(128)}) while((s32[]{:T(128)}, bf16[2,16,32,8192]{3,2,1,0:T(8,128)(2,1)}, s32[12,4]{0,1:T(4,128)S(1)}, bf16[12,2,16,32,256]{4,3,2,0,1:T(8,128)(2,1)}, s32[]{:T(128)}) %tuple.20), condition=%wide.while_cond, body=%wide.while_body.sunk | while | flops 2 | bytes 1049705 | solution.py:81
  450.2 21.0 %copy.72 = bf16[2,12,16,32,256]{3,4,2,1,0:T(8,128)(2,1)} copy(bf16[2,12,16,32,256]{4,3,2,1,0:T(8,128)(2,1)} %pad_maximum_fusion) | data formatting | bytes 12582912 | tf_op jit(solution)/shard_map/stack | solution.py:88
  471.2 54.6 %copy.73 = bf16[16,2,12,32,16,16]{5,4,3,2,1,0:T(8,128)(2,1)} copy(bf16[16,2,12,32,16,16]{3,5,0,4,2,1:T(8,128)(2,1)} %bitcast.110) | data formatting | bytes 12582912 | tf_op jit(solution)/shard_map/transpose | solution.py:94
  525.8 45.0 %reshape_reshape.3 = bf16[16,196608]{1,0:T(8,128)(2,1)} reshape(bf16[16,2,12,32,16,16]{5,4,3,2,1,0:T(8,128)(2,1)} %copy.73) | data formatting | bytes 12582912 | tf_op jit(solution)/shard_map/reshape;reshape | solution.py:106
  570.8 11.8 %convolution_convert_fusion = bf16[48,196608]{1,0:T(8,128)(2,1)} fusion(bf16[16,196608]{1,0:T(8,128)(2,1)} %reshape_reshape.3, s32[16]{0:T(128)S(1)} %multiply_add_fusion), kind=kOutput, calls=%fused_computation.2 | convolution fusion | flops 311427840 | bytes 25165888 | tf_op jit(solution)/shard_map/dot_general | solution.py:105
  582.6 11.5 %copy.82 = bf16[6,8,768,256]{3,2,1,0:T(8,128)(2,1)S(1)} copy(bf16[6,8,768,256]{3,1,2,0:T(8,128)(2,1)} %bitcast.111) | data formatting | bytes 37748736
  594.1 208.6 %all_to_all.30 = bf16[4,12,2,12,32,256]{5,4,3,2,1,0:T(8,128)(2,1)S(1)} all-to-all(bf16[4,12,2,12,32,256]{5,4,3,2,1,0:T(8,128)(2,1)S(1)} %bitcast.112), channel_id=1, replica_groups=mesh['rx'=4,'chirp'=8] {'rx'}, dimensions={0} | all-to-all | bytes 37748736 | tf_op jit(solution)/shard_map/all_to_all | solution.py:109
  802.6 6.6 copy.74
  809.2 8.2 fusion.1
  822.0 4.4 fusion.24
  (69 shorter events, 59.5 us)
Async XLA Ops:
  8.3 7.0 copy-start.6
  8.3 7.2 copy-start.5
  8.3 190.4 %all-to-all-start = ((bf16[2,128,32,512]{3,2,0,1:T(8,128)(2,1)}), bf16[2,128,32,512]{3,2,0,1:T(8,128)(2,1)}, u32[]{:S(2)}, u32[]{:S(2)}) async-start(bf16[2,128,32,512]{3,2,0,1:T(8,128)(2,1)} %copy.56), calls=%async_computation | async-start | bytes 16777216 | tf_op jit(solution)/shard_map/all_to_all | solution.py:69
  243.4 6.9 copy-start.1
  278.1 6.9 copy-start
  303.2 8.8 %copy-start.2 = (bf16[512,64,64]{0,1,2:T(8,128)(2,1)S(1)}, bf16[512,64,64]{0,1,2:T(8,128)(2,1)}, u32[]{:S(2)}) copy-start(bf16[512,64,64]{0,1,2:T(8,128)(2,1)} %get-tuple-element.21) | copy-start | bytes 12582916
  802.6 6.6 copy-start.4
  809.2 10.2 %copy-start.3 = (bf16[4,12,2,12,32,256]{5,4,0,3,2,1:T(8,128)(2,1)S(1)}, bf16[4,12,2,12,32,256]{5,4,0,3,2,1:T(8,128)(2,1)}, u32[]{:S(2)}) copy-start(bf16[4,12,2,12,32,256]{5,4,0,3,2,1:T(8,128)(2,1)} %copy.74) | copy-start | bytes 56623108
where the time goes:
time: 846 us; the launch traced here: 832 us
  local copies, waits for them, and re-layouts  317 us (37%)
  blocking collectives  209 us (25%)
  waiting for transfers between devices  183 us (22%)
  matrix products  95.2 us (11%)
  other arithmetic  22.2 us (3%)
    all_to_all x1, blocking collectives, shards(): lax.all_to_all(outgoing, 'rx', split_axis=0, concat_axis=4, tiled=True)[0]  209 us
    all_to_all x1, waiting for transfers between devices, shards(): lax.all_to_all(samples, 'chirp', split_axis=1, concat_axis=3, tiled=True)  183 us
    transpose x1, local copies, waits for them, and re-layouts, shards(): tiles.transpose(4, 0, 1, 2, 3, 5)  54.6 us
    another operation x1, local copies, waits for them, and re-layouts, shards(): tiles.reshape(band_count, -1)  45 us
    gather x36, local copies, waits for them, and re-layouts  41 us
    convert_element_type x2, local copies, waits for them, and re-layouts, spectrum_of(): out_im.reshape(row_count, K1 * K2).astype(jnp.bfloat16)  28.1 us
    convert_element_type x2, local copies, waits for them, and re-layouts, spectrum_of(): out_re.reshape(row_count, K1 * K2).astype(jnp.bfloat16)  27.7 us
    another operation x2, local copies, waits for them, and re-layouts, spectrum_of(): split_im = imag_part.reshape(row_count, K1, K2)  23.4 us
  transfers between devices with their start and end apart: 1, of which 1 were waited for; matrix products, arithmetic and copies ran while one was open for 0% of the time, Pallas kernels for 0%

commit v1 on v0

--- a/solution.py
+++ b/solution.py
@@ -4,6 +4,8 @@
 import jax
 import jax.numpy as jnp
 from jax import lax
+from jax.experimental import pallas as pl
+from jax.experimental.pallas import tpu as pltpu
 from jax.sharding import PartitionSpec as P
 
 K1 = 64
@@ -52,7 +54,7 @@
     )
 
 
-def shards(samples, tx_offsets, band_owner, beam_weights):
+def general(samples, tx_offsets, band_owner, beam_weights):
     owners = lax.axis_size("rx")
     band_count = band_owner.shape[0]
     capacity = 3 * band_count // owners
@@ -119,6 +121,293 @@
     return jnp.stack([beam_re, beam_im], axis=1).astype(jnp.bfloat16)
 
 
+LANES = 128
+GROUPS = 32
+
+
+def fourier_of_8(re, im):
+    half = math.sqrt(0.5)
+
+    def fourier_of_4(a, b, c, d):
+        s0, s1 = (a[0] + c[0], a[1] + c[1]), (a[0] - c[0], a[1] - c[1])
+        s2, s3 = (b[0] + d[0], b[1] + d[1]), (b[0] - d[0], b[1] - d[1])
+        return (
+            (s0[0] + s2[0], s0[1] + s2[1]),
+            (s1[0] + s3[1], s1[1] - s3[0]),
+            (s0[0] - s2[0], s0[1] - s2[1]),
+            (s1[0] - s3[1], s1[1] + s3[0]),
+        )
+
+    x = list(zip(re, im))
+    even = fourier_of_4(x[0], x[2], x[4], x[6])
+    odd = fourier_of_4(x[1], x[3], x[5], x[7])
+    o1 = ((odd[1][0] + odd[1][1]) * half, (odd[1][1] - odd[1][0]) * half)
+    o3 = ((odd[3][1] - odd[3][0]) * half, -(odd[3][0] + odd[3][1]) * half)
+    turned = (odd[0], o1, (odd[2][1], -odd[2][0]), o3)
+    first = [(e[0] + o[0], e[1] + o[1]) for e, o in zip(even, turned)]
+    second = [(e[0] - o[0], e[1] - o[1]) for e, o in zip(even, turned)]
+    return first + second
+
+
+def beams_kernel(
+    chunk_bins, rows, slot_ids, x_ref, table_ref, weight_ref, out_ref, part, mixed, spread, masked
+):
+    sources = x_ref.shape[0]
+    folds = x_ref.shape[4] // LANES
+    tx2 = spread.shape[0]
+    halves = rows // 16
+
+    def transform(step, carry):
+        q = step // halves
+        r0 = pl.multiple_of((step % halves) * 16, 16)
+        for fold in range(folds):
+            re = [
+                x_ref[c, 0, q, pl.ds(r0, 16), fold * LANES : (fold + 1) * LANES].astype(jnp.float32)
+                for c in range(sources)
+            ]
+            im = [
+                x_ref[c, 1, q, pl.ds(r0, 16), fold * LANES : (fold + 1) * LANES].astype(jnp.float32)
+                for c in range(sources)
+            ]
+            for k, (a, b) in enumerate(fourier_of_8(re, im)):
+                angle = -2.0 * math.pi * fold * k / GROUPS
+                if fold * k:
+                    c, s = math.cos(angle), math.sin(angle)
+                    a, b = a * c - b * s, a * s + b * c
+                part[fold, k, 0] = a
+                part[fold, k, 1] = b
+        base = pl.multiple_of(q * rows + r0, 16)
+        for k in range(sources):
+            v = [(part[f, k, 0], part[f, k, 1]) for f in range(folds)]
+            s0, s1 = (v[0][0] + v[2][0], v[0][1] + v[2][1]), (v[0][0] - v[2][0], v[0][1] - v[2][1])
+            s2, s3 = (v[1][0] + v[3][0], v[1][1] + v[3][1]), (v[1][0] - v[3][0], v[1][1] - v[3][1])
+            outs = (
+                (s0[0] + s2[0], s0[1] + s2[1]),
+                (s1[0] + s3[1], s1[1] - s3[0]),
+                (s0[0] - s2[0], s0[1] - s2[1]),
+                (s1[0] - s3[1], s1[1] + s3[0]),
+            )
+            for f, (a, b) in enumerate(outs):
+                mixed[k + sources * f, pl.ds(base, 16), :LANES] = a.astype(jnp.bfloat16)
+                mixed[k + sources * f, pl.ds(base, 16), LANES:] = b.astype(jnp.bfloat16)
+        return carry
+
+    lax.fori_loop(0, chunk_bins * halves, transform, 0)
+
+    def demultiplex(group, carry):
+        got = lax.dot_general(
+            table_ref[group], mixed[group], (((1,), (1,)), ((), ())),
+            preferred_element_type=jnp.float32,
+        )
+        for t in range(tx2):
+            spread[t, pl.ds(group, 8, stride=GROUPS), :] = got[8 * t : 8 * t + 8]
+        return carry
+
+    lax.fori_loop(0, GROUPS, demultiplex, 0, unroll=4)
+
+    lane_bin = lax.broadcasted_iota(jnp.int32, (16, LANES), 1) // rows
+    for t in range(tx2):
+        def scatter(band, carry):
+            at = pl.multiple_of(band * 16, 16)
+            tile = spread[t, pl.ds(at, 16), :]
+            for q in range(chunk_bins):
+                kept = jnp.where(lane_bin == q, tile, 0.0).astype(jnp.bfloat16)
+                to = pl.multiple_of((band * chunk_bins + q) * 16, 16)
+                masked[pl.ds(to, 16), t * LANES : (t + 1) * LANES] = kept
+            return carry
+
+        lax.fori_loop(0, 16, scatter, 0, unroll=4)
+
+    low = lax.broadcasted_iota(jnp.int32, (256, LANES), 1) < LANES // 2
+
+    def combine(block, carry):
+        at = pl.multiple_of(block * 256, 256)
+        beams = lax.dot_general(
+            weight_ref[...], masked[pl.ds(at, 256), :], (((1,), (1,)), ((), ())),
+            preferred_element_type=jnp.float32,
+        )
+        for pair in range(2):
+            top = beams[:256, pair * LANES : (pair + 1) * LANES]
+            bottom = beams[256:, pair * LANES : (pair + 1) * LANES]
+            even = jnp.where(low, top, pltpu.roll(bottom, LANES // 2, 1))
+            odd = jnp.where(low, pltpu.roll(top, LANES // 2, 1), bottom)
+            out_ref[slot_ids[4 * block + 2 * pair]] = even.astype(jnp.bfloat16)
+            out_ref[slot_ids[4 * block + 2 * pair + 1]] = odd.astype(jnp.bfloat16)
+        return carry
+
+    lax.fori_loop(0, 4, combine, 0)
+
+
+def beams_of(slot_ids, chunk, table, weights, slots):
+    sources, _, chunk_bins, rows, _ = chunk.shape
+    tx2 = table.shape[1] // 8
+    vmem = pl.BlockSpec(memory_space=pltpu.VMEM)
+    return pl.pallas_call(
+        partial(beams_kernel, chunk_bins, rows),
+        out_shape=jax.ShapeDtypeStruct((slots, 256, LANES), jnp.bfloat16),
+        in_specs=[pl.BlockSpec(memory_space=pltpu.SMEM), vmem, vmem, vmem],
+        out_specs=vmem,
+        scratch_shapes=[
+            pltpu.VMEM((4, 8, 2, 16, LANES), jnp.float32),
+            pltpu.VMEM((GROUPS, LANES, 2 * LANES), jnp.bfloat16),
+            pltpu.VMEM((tx2, 256, LANES), jnp.float32),
+            pltpu.VMEM((1024, tx2 * LANES), jnp.bfloat16),
+        ],
+        compiler_params=pltpu.CompilerParams(vmem_limit_bytes=56 << 20),
+        name="beams",
+    )(slot_ids, chunk, table, weights)
+
+
+def store_kernel(taken, *refs):
+    *pieces, out_ref = refs
+    slot = pl.program_id(0)
+    used = slot < taken[0]
+    low = lax.broadcasted_iota(jnp.int32, (256, LANES), 1) < LANES // 2
+    sums = []
+    for side in range(2):
+        group = pieces[4 * side : 4 * side + 4]
+        total = group[0][...].reshape(256, LANES).astype(jnp.float32)
+        for ref in group[1:]:
+            total = total + ref[...].reshape(256, LANES).astype(jnp.float32)
+        sums.append(jnp.where(used, total, 0.0))
+    first = jnp.where(low, sums[0], pltpu.roll(sums[1], LANES // 2, 1)).astype(jnp.bfloat16)
+    second = jnp.where(low, pltpu.roll(sums[0], LANES // 2, 1), sums[1]).astype(jnp.bfloat16)
+    out_ref[0, 0, :128, :] = first[:128]
+    out_ref[0, 1, :128, :] = first[128:]
+    out_ref[0, 0, 128:, :] = second[:128]
+    out_ref[0, 1, 128:, :] = second[128:]
+
+
+def store_pair(taken, me, left, right, so_far, pair, capacity):
+    own = pl.BlockSpec((1, 1, 256, LANES), lambda s, taken, me: (me[0], s, 0, 0))
+    got = pl.BlockSpec((1, 256, LANES), lambda s, taken, me: (s, 0, 0))
+    specs = ([own] + [got] * 3) * 2
+    args = [*left, *right]
+    aliases = {}
+    if so_far is not None:
+        specs.append(pl.BlockSpec(memory_space=pl.ANY))
+        args.append(so_far)
+        aliases = {2 + 8: 0}
+
+    def body(taken, me, *refs):
+        store_kernel(taken, *refs[:8], refs[-1])
+
+    return pl.pallas_call(
+        body,
+        out_shape=jax.ShapeDtypeStruct((capacity, 2, 256, 2 * LANES), jnp.bfloat16),
+        grid_spec=pltpu.PrefetchScalarGridSpec(
+            num_scalar_prefetch=2,
+            grid=(capacity,),
+            in_specs=specs,
+            out_specs=pl.BlockSpec((1, 2, 256, LANES), lambda s, taken, me: (s, 0, 0, pair)),
+        ),
+        input_output_aliases=aliases,
+        name="store",
+    )(taken, me, *args)
+
+
+def tuned(samples, tx_offsets, band_owner, beam_weights):
+    owners = lax.axis_size("rx")
+    spans = lax.axis_size("chirp")
+    me = lax.axis_index("rx")
+    bands = band_owner.shape[0]
+    tx_count = tx_offsets.shape[0]
+    capacity = 3 * bands // owners
+    rows = samples.shape[2]
+    bins = samples.shape[1] // spans
+    chunk_bins = LANES // rows
+    chunks = bins // chunk_bins
+    slots = owners * capacity
+
+    counter = jnp.arange(bands, dtype=jnp.int32)
+    same_owner = band_owner[:, None] == band_owner[None, :]
+    earlier = counter[None, :] < counter[:, None]
+    band_rank = jnp.sum((same_owner & earlier).astype(jnp.int32), axis=1)
+    slot_ids = band_owner * capacity + band_rank
+    taken = jnp.sum((band_owner == me).astype(jnp.int32)).reshape(1)
+
+    split = samples.reshape(2, spans, chunks, chunk_bins, rows, samples.shape[3])
+    chunk_in = [split[:, :, i].transpose(1, 0, 2, 3, 4) for i in range(chunks)]
+
+    two_pi = 2.0 * math.pi
+    group = jnp.arange(GROUPS, dtype=jnp.int32)
+    high = jnp.arange(8, dtype=jnp.int32)
+    lane = jnp.arange(LANES, dtype=jnp.int32)
+    sender = jnp.arange(tx_count, dtype=jnp.int32)
+    start = tx_offsets[:, None] + 32 * high[None, :] + 4096 - 128
+    a1 = (start[:, :, None] * lane % 4096).astype(jnp.float32) * (-two_pi / 4096)
+    a2 = (group[:, None] * lane[None, :]).astype(jnp.float32) * (-two_pi / 4096)
+    speed = 32 * high[None, :] + group[:, None] - 128
+    a3 = (sender[None, :, None] * speed[:, None, :]).astype(jnp.float32) * (
+        -two_pi / (tx_count * 256)
+    )
+    c1, s1 = lax.optimization_barrier((jnp.cos(a1), jnp.sin(a1)))
+    c2, s2 = lax.optimization_barrier((jnp.cos(a2) / 64, jnp.sin(a2) / 64))
+    c3, s3 = lax.optimization_barrier((jnp.cos(a3), jnp.sin(a3)))
+    c2, s2 = c2[:, None, None, :], s2[:, None, None, :]
+    c3, s3 = c3[..., None], s3[..., None]
+    c12, s12 = c1 * c2 - s1 * s2, c1 * s2 + s1 * c2
+    turn_re = (c12 * c3 - s12 * s3).reshape(GROUPS, tx_count * 8, LANES)
+    turn_im = (c12 * s3 + s12 * c3).reshape(GROUPS, tx_count * 8, LANES)
+    table = jnp.concatenate(
+        [
+            jnp.concatenate([turn_re, -turn_im], axis=2),
+            jnp.concatenate([turn_im, turn_re], axis=2),
+        ],
+        axis=1,
+    ).astype(jnp.bfloat16)
+
+    local = lax.dynamic_slice_in_dim(
+        beam_weights.reshape(2, 2, 128, tx_count, owners * rows), me * rows, rows, 4
+    )
+    local = jnp.tile(local, (1, 1, 1, 1, chunk_bins))
+    local = local.reshape(2, 2, 128, tx_count * LANES)
+    weights = jnp.stack(
+        [
+            jnp.concatenate([local[0], -local[1]], axis=2),
+            jnp.concatenate([local[1], local[0]], axis=2),
+        ],
+        axis=1,
+    ).reshape(512, 2 * tx_count * LANES)
+
+    swaps = [[(i, i ^ k) for i in range(owners)] for k in range(owners)]
+    shares = [None] * chunks
+    arrived = [None] * chunks
+    for i in range(chunks):
+        piece = chunk_in[i]
+        if i >= 2:
+            piece, shares[i - 2] = lax.optimization_barrier((piece, shares[i - 2]))
+        arrived[i] = lax.all_to_all(piece, "chirp", split_axis=0, concat_axis=0, tiled=True)
+        if i >= 1:
+            shares[i - 1] = beams_of(slot_ids, arrived[i - 1], table, weights, slots)
+    shares[-1] = beams_of(slot_ids, arrived[-1], table, weights, slots)
+
+    groups = []
+    for i in range(chunks):
+        whole = shares[i].reshape(owners, capacity, 256, LANES)
+        got = [
+            lax.ppermute(lax.dynamic_index_in_dim(whole, me ^ k, 0, keepdims=False), "rx", swaps[k])
+            for k in range(1, owners)
+        ]
+        groups.append([whole] + got)
+    store = None
+    for pair in range(chunks // 2):
+        store = store_pair(
+            taken, me.reshape(1), groups[2 * pair], groups[2 * pair + 1], store, pair, capacity
+        )
+    return store
+
+
+def shards(samples, tx_offsets, band_owner, beam_weights):
+    fits = (
+        lax.axis_size("rx") == 4
+        and lax.axis_size("chirp") == 8
+        and samples.shape == (2, 128, 32, 512)
+        and beam_weights.shape == (2, 256, 1536)
+    )
+    return (tuned if fits else general)(samples, tx_offsets, band_owner, beam_weights)
+
+
 def solution(mesh):
     placed = (P(None, None, "rx", "chirp"), P(), P(), P())
     return jax.shard_map(

time: 846 us -> 327 us (0.39); the launches traced: 832 us -> 326 us
  local copies, waits for them, and re-layouts: 317 us -> 30.2 us
  blocking collectives: 209 us -> 0 us
  matrix products: 95.2 us -> 0 us
  Pallas kernels: 0 us -> 85.6 us
  starting transfers between devices: 6.49 us -> 35.5 us
  other arithmetic: 22.2 us -> 5.65 us
  waiting for transfers between devices: 183 us -> 169 us
    all_to_all x1 -> x0, blocking collectives: 209 us -> none  [shards(): lax.all_to_all(outgoing, 'rx', split_axis=0, concat_axis=4, tiled=True)[0]]
    another operation x8 -> x3, local copies, waits for them, and re-layouts: 115 us -> 3.06 us  [the longest x1 2.82 us: tuned(): jnp.stack([jnp.concatenate([local[0], -local[1]], axis=2), jnp.concatenat...]
    dot_general x13 -> x0, matrix products: 95.2 us -> none  [the longest x1 12.6 us: spectrum_of(): mixing('kn,rnm->rkm', table_re, split_re)]
    pallas_call x0 -> x6, Pallas kernels: none -> 85.6 us  [the longest x4 66.9 us: beams_of(): pl.pallas_call(partial(beams_kernel, chunk_bins, rows), out_shape=jax.Sha...]
    all_to_all x1 -> x4, waiting for transfers between devices: 183 us -> 103 us  [tuned(): lax.all_to_all(piece, 'chirp', split_axis=0, concat_axis=0, tiled=True)]
    ppermute x0 -> x12, waiting for transfers between devices: none -> 65.9 us  [tuned(): lax.ppermute(lax.dynamic_index_in_dim(whole, me ^ k, 0, keepdims=False),...]
    convert_element_type x4 -> x0, local copies, waits for them, and re-layouts: 55.8 us -> none  [the longest x2 28.1 us: spectrum_of(): out_im.reshape(row_count, K1 * K2).astype(jnp.bfloat16)]
    transpose x1, local copies, waits for them, and re-layouts: 54.6 us -> 2.26 us  [tuned(): chunk_in = [split[:, :, i].transpose(1, 0, 2, 3, 4) for i in range(chunks)]]
  transfers between devices with their start and end apart: 1 -> 16, of which waited for: 1 -> 12; matrix products, arithmetic and copies ran while one was open for 0% -> 8% of each run, Pallas kernels for 0% -> 23%
where the time goes in v1:
time: 327 us; the launch traced here: 326 us
  waiting for transfers between devices  169 us (52%)
  Pallas kernels  85.6 us (26%)
  starting transfers between devices  35.5 us (11%)
  local copies, waits for them, and re-layouts  30.2 us (9%)
  other arithmetic  5.65 us (2%)
    all_to_all x4, waiting for transfers between devices, tuned(): lax.all_to_all(piece, 'chirp', split_axis=0, concat_axis=0, tiled=True)  103 us
    pallas_call x4, Pallas kernels, beams_of(): pl.pallas_call(partial(beams_kernel, chunk_bins, rows), out_shape=jax.Sha...  66.9 us
    ppermute x12, waiting for transfers between devices, tuned(): lax.ppermute(lax.dynamic_index_in_dim(whole, me ^ k, 0, keepdims=False),...  65.9 us
    all_to_all x4, starting transfers between devices, tuned(): lax.all_to_all(piece, 'chirp', split_axis=0, concat_axis=0, tiled=True)  19.6 us
    pallas_call x2, Pallas kernels, store_pair(): pl.pallas_call(body, out_shape=jax.ShapeDtypeStruct((capacity, 2, 256, 2...  18.6 us
    ppermute x12, starting transfers between devices, tuned(): lax.ppermute(lax.dynamic_index_in_dim(whole, me ^ k, 0, keepdims=False),...  15.9 us
    unnamed x29, local copies, waits for them, and re-layouts  9.36 us
    squeeze x4, local copies, waits for them, and re-layouts, tuned(): lax.dynamic_index_in_dim(whole, me ^ k, 0, keepdims=False)  8.88 us
  transfers between devices with their start and end apart: 16, of which 12 were waited for; matrix products, arithmetic and copies ran while one was open for 8% of the time, Pallas kernels for 23%

profile of v1, /device:TPU:0, one launch (start us, length us, event | category | flops | bytes accessed | tf_op | source)
XLA Modules:
  0.0 325.7 jit_solution(6801282076766451470)
XLA Ops:
  0.0 5.7 %fusion.13 = (bf16[2,8,1,4,32,512]{5,4,3,2,1,0:T(8,128)(2,1)S(1)}, bf16[2,8,1,4,32,512]{5,4,3,2,1,0:T(8,128)(2,1)}, bf16[2,8,1,4,32,512]{5,4,3,2,1,0:T(8,128)(2,1)}, bf16[2,8,1,4,32,512]{5,4,3,2,1,0:T(8,128)(2,1)}) fusion(bf16[2,8,4,4,32,512]{5,4,3,2,1,0:T(8,128)(2,1)} %bitcast.79), kind=kLoop, calls=%fused_computation.55 | loop fusion | bytes 16777216 | tf_op jit(solution)/shard_map/slice | solution.py:330
  5.7 1.6 copy.35
  7.3 6.3 %all-to-all-start.2 = ((bf16[8,2,4,32,512]{4,3,2,1,0:T(8,128)(2,1)}), bf16[8,2,4,32,512]{4,3,2,1,0:T(8,128)(2,1)S(1)}, u32[]{:S(2)}, u32[]{:S(2)}) async-start(bf16[8,2,4,32,512]{4,3,2,1,0:T(8,128)(2,1)} %bitcast.65), calls=%async_computation.2 | async-start | bytes 4194304 | tf_op jit(solution)/shard_map/all_to_all | solution.py:380
  13.7 3.2 copy.36
  16.9 45.8 %all-to-all-done.2.x_ref = bf16[8,2,4,32,512]{4,3,2,1,0:T(8,128)(2,1)S(1)} async-done(((bf16[8,2,4,32,512]{4,3,2,1,0:T(8,128)(2,1)}), bf16[8,2,4,32,512]{4,3,2,1,0:T(8,128)(2,1)S(1)}, u32[]{:S(2)}, u32[]{:S(2)}) %all-to-all-start.2) | async-done | bytes 2097184 | tf_op jit(solution)/shard_map/all_to_all | solution.py:380
  64.0 4.4 %all-to-all-start = ((bf16[8,2,4,32,512]{4,3,2,1,0:T(8,128)(2,1)}), bf16[8,2,4,32,512]{4,3,2,1,0:T(8,128)(2,1)}, u32[]{:S(2)}, u32[]{:S(2)}) async-start(bf16[8,2,4,32,512]{4,3,2,1,0:T(8,128)(2,1)} %bitcast.66), calls=%async_computation | async-start | bytes 4194304 | tf_op jit(solution)/shard_map/all_to_all | solution.py:380
  68.4 1.7 copy.21
  71.8 2.8 copy.24
  78.0 1.9 maximum_maximum_fusion.table_ref
  81.3 2.3 copy_bitcast_fusion.1
  83.6 16.7 %beams.6 = bf16[48,256,128]{2,1,0:T(8,128)(2,1)} custom-call(s32[16]{0:T(128)} %get-tuple-element.52.slot_ids, bf16[8,2,4,32,512]{4,3,2,1,0:T(8,128)(2,1)} %copy-done.2, bf16[32,192,256]{2,1,0:T(8,128)(2,1)} %maximum_maximum_fusion.table_ref, bf16[512,3072]{1,0:T(8,128)(2,1)} %bitcast.67), custom_call_target="tpu_custom_call" | custom-call | tf_op jit(solution)/shard_map/beams/pallas_call | solution.py:245
  100.3 17.1 %all-to-all-done.x_ref = bf16[8,2,4,32,512]{4,3,2,1,0:T(8,128)(2,1)} async-done(((bf16[8,2,4,32,512]{4,3,2,1,0:T(8,128)(2,1)}), bf16[8,2,4,32,512]{4,3,2,1,0:T(8,128)(2,1)}, u32[]{:S(2)}, u32[]{:S(2)}) %all-to-all-start) | async-done | bytes 2097184 | tf_op jit(solution)/shard_map/all_to_all | solution.py:380
  117.4 4.3 %all-to-all-start.3 = ((bf16[8,2,4,32,512]{4,3,2,1,0:T(8,128)(2,1)}), bf16[8,2,4,32,512]{4,3,2,1,0:T(8,128)(2,1)}, u32[]{:S(2)}, u32[]{:S(2)}) async-start(bf16[8,2,4,32,512]{4,3,2,1,0:T(8,128)(2,1)} %get-tuple-element.22), calls=%async_computation.3 | async-start | bytes 4194304 | tf_op jit(solution)/shard_map/all_to_all | solution.py:380
  121.8 16.7 %beams.4 = bf16[48,256,128]{2,1,0:T(8,128)(2,1)} custom-call(s32[16]{0:T(128)} %get-tuple-element.52.slot_ids, bf16[8,2,4,32,512]{4,3,2,1,0:T(8,128)(2,1)} %all-to-all-done.x_ref, bf16[32,192,256]{2,1,0:T(8,128)(2,1)} %maximum_maximum_fusion.table_ref, bf16[512,3072]{1,0:T(8,128)(2,1)} %bitcast.68), custom_call_target="tpu_custom_call" | custom-call | tf_op jit(solution)/shard_map/beams/pallas_call | solution.py:245
  138.5 32.3 %all-to-all-done.3.x_ref = bf16[8,2,4,32,512]{4,3,2,1,0:T(8,128)(2,1)} async-done(((bf16[8,2,4,32,512]{4,3,2,1,0:T(8,128)(2,1)}), bf16[8,2,4,32,512]{4,3,2,1,0:T(8,128)(2,1)}, u32[]{:S(2)}, u32[]{:S(2)}) %all-to-all-start.3) | async-done | bytes 2097184 | tf_op jit(solution)/shard_map/all_to_all | solution.py:380
  170.8 4.5 %all-to-all-start.1 = ((bf16[8,2,4,32,512]{4,3,2,1,0:T(8,128)(2,1)}), bf16[8,2,4,32,512]{4,3,2,1,0:T(8,128)(2,1)}, u32[]{:S(2)}, u32[]{:S(2)}) async-start(bf16[8,2,4,32,512]{4,3,2,1,0:T(8,128)(2,1)} %get-tuple-element.21), calls=%async_computation.1 | async-start | bytes 4194304 | tf_op jit(solution)/shard_map/all_to_all | solution.py:380
  184.5 16.7 %beams.7 = bf16[48,256,128]{2,1,0:T(8,128)(2,1)} custom-call(s32[16]{0:T(128)} %get-tuple-element.52.slot_ids, bf16[8,2,4,32,512]{4,3,2,1,0:T(8,128)(2,1)} %all-to-all-done.3.x_ref, bf16[32,192,256]{2,1,0:T(8,128)(2,1)} %maximum_maximum_fusion.table_ref, bf16[512,3072]{1,0:T(8,128)(2,1)} %bitcast.69), custom_call_target="tpu_custom_call" | custom-call | tf_op jit(solution)/shard_map/beams/pallas_call | solution.py:245
  201.2 3.2 dynamic-slice_bitcast_fusion.6
  204.4 9.4 %collective-permute-done.10.refs_6_ = bf16[12,256,128]{2,1,0:T(8,128)(2,1)S(1)} collective-permute-done((bf16[12,256,128]{2,1,0:T(8,128)(2,1)S(1)}, bf16[12,256,128]{2,1,0:T(8,128)(2,1)S(1)}, u32[]{:S(2)}, u32[]{:S(2)}) %collective-permute-start.10) | collective-permute-done | bytes 786464 | tf_op jit(solution)/shard_map/ppermute | solution.py:389
  213.7 2.4 collective-permute-start.8
  216.7 7.5 %all-to-all-done.1.x_ref = bf16[8,2,4,32,512]{4,3,2,1,0:T(8,128)(2,1)} async-done(((bf16[8,2,4,32,512]{4,3,2,1,0:T(8,128)(2,1)}), bf16[8,2,4,32,512]{4,3,2,1,0:T(8,128)(2,1)}, u32[]{:S(2)}, u32[]{:S(2)}) %all-to-all-start.1) | async-done | bytes 2097184 | tf_op jit(solution)/shard_map/all_to_all | solution.py:380
  224.2 16.7 %beams.5 = bf16[48,256,128]{2,1,0:T(8,128)(2,1)} custom-call(s32[16]{0:T(128)} %get-tuple-element.52.slot_ids, bf16[8,2,4,32,512]{4,3,2,1,0:T(8,128)(2,1)} %all-to-all-done.1.x_ref, bf16[32,192,256]{2,1,0:T(8,128)(2,1)} %maximum_maximum_fusion.table_ref, bf16[512,3072]{1,0:T(8,128)(2,1)} %bitcast.70), custom_call_target="tpu_custom_call" | custom-call | tf_op jit(solution)/shard_map/beams/pallas_call | solution.py:245
  240.9 3.1 dynamic-slice_bitcast_fusion.9
  247.5 2.4 collective-permute-done.8.refs_3_
  250.5 15.4 %collective-permute-done.3.refs_5_ = bf16[12,256,128]{2,1,0:T(8,128)(2,1)} collective-permute-done((bf16[12,256,128]{2,1,0:T(8,128)(2,1)}, bf16[12,256,128]{2,1,0:T(8,128)(2,1)}, u32[]{:S(2)}, u32[]{:S(2)}) %collective-permute-start.3) | collective-permute-done | bytes 786464 | tf_op jit(solution)/shard_map/ppermute | solution.py:389
  265.8 2.4 collective-permute-start.2
  268.3 9.3 %store.2.refs_8_ = bf16[12,2,256,256]{3,2,1,0:T(8,128)(2,1)} custom-call(s32[1]{0:T(128)} %bitcast.taken, s32[1]{0:T(128)} %bitcast.1.me, bf16[4,12,256,128]{3,2,1,0:T(8,128)(2,1)} %bitcast.73, bf16[12,256,128]{2,1,0:T(8,128)(2,1)} %copy-done.8, bf16[12,256,128]{2,1,0:T(8,128)(2,1)} %collective-permute-done.7.refs_2_, ...), custom_call_target="tpu_custom_call" | custom-call | tf_op jit(solution)/shard_map/store/pallas_call | solution.py:295
  277.6 2.5 collective-permute-done.4.refs_6_
  280.1 3.5 %collective-permute-done.5.refs_7_ = bf16[12,256,128]{2,1,0:T(8,128)(2,1)S(1)} collective-permute-done((bf16[12,256,128]{2,1,0:T(8,128)(2,1)}, bf16[12,256,128]{2,1,0:T(8,128)(2,1)S(1)}, u32[]{:S(2)}, u32[]{:S(2)}) %collective-permute-start.5) | collective-permute-done | bytes 786464 | tf_op jit(solution)/shard_map/ppermute | solution.py:389
  283.6 16.0 %collective-permute-done.refs_1_ = bf16[12,256,128]{2,1,0:T(8,128)(2,1)} collective-permute-done((bf16[12,256,128]{2,1,0:T(8,128)(2,1)}, bf16[12,256,128]{2,1,0:T(8,128)(2,1)}, u32[]{:S(2)}, u32[]{:S(2)}) %collective-permute-start) | collective-permute-done | bytes 786464 | tf_op jit(solution)/shard_map/ppermute | solution.py:389
  300.5 15.9 %collective-permute-done.2.refs_3_ = bf16[12,256,128]{2,1,0:T(8,128)(2,1)} collective-permute-done((bf16[12,256,128]{2,1,0:T(8,128)(2,1)}, bf16[12,256,128]{2,1,0:T(8,128)(2,1)}, u32[]{:S(2)}, u32[]{:S(2)}) %collective-permute-start.2) | collective-permute-done | bytes 786464 | tf_op jit(solution)/shard_map/ppermute | solution.py:389
  316.4 9.3 %store.3 = bf16[12,2,256,256]{3,2,1,0:T(8,128)(2,1)} custom-call(s32[1]{0:T(128)} %bitcast.taken, s32[1]{0:T(128)} %bitcast.1.me, bf16[4,12,256,128]{3,2,1,0:T(8,128)(2,1)} %bitcast.78, bf16[12,256,128]{2,1,0:T(8,128)(2,1)} %collective-permute-done.refs_1_, bf16[12,256,128]{2,1,0:T(8,128)(2,1)} %collective-permute-done.1.refs_2_, ...), custom_call_target="tpu_custom_call", output_to_operand_aliasing={{}: (10, {})} | custom-call | tf_op jit(solution)/shard_map/store/pallas_call | solution.py:295
  (63 shorter events, 22.2 us)
Async XLA Ops:
  7.3 55.4 %all-to-all-start.2 = ((bf16[8,2,4,32,512]{4,3,2,1,0:T(8,128)(2,1)}), bf16[8,2,4,32,512]{4,3,2,1,0:T(8,128)(2,1)S(1)}, u32[]{:S(2)}, u32[]{:S(2)}) async-start(bf16[8,2,4,32,512]{4,3,2,1,0:T(8,128)(2,1)} %bitcast.65), calls=%async_computation.2 | async-start | bytes 4194304 | tf_op jit(solution)/shard_map/all_to_all | solution.py:380
  62.7 1.3 copy-start.2
  64.0 53.4 %all-to-all-start = ((bf16[8,2,4,32,512]{4,3,2,1,0:T(8,128)(2,1)}), bf16[8,2,4,32,512]{4,3,2,1,0:T(8,128)(2,1)}, u32[]{:S(2)}, u32[]{:S(2)}) async-start(bf16[8,2,4,32,512]{4,3,2,1,0:T(8,128)(2,1)} %bitcast.66), calls=%async_computation | async-start | bytes 4194304 | tf_op jit(solution)/shard_map/all_to_all | solution.py:380
  71.8 3.2 copy-start.11
  71.8 3.7 %copy-start.12 = (s32[16]{0:T(128)S(1)}, s32[16]{0:T(128)}, u32[]{:S(2)}) copy-start(s32[16]{0:T(128)} %param.6) | copy-start | bytes 196
  77.9 2.5 copy-start.3
  78.0 3.4 %copy-start.4 = (bf16[2,8,1,4,32,512]{5,4,3,2,1,0:T(8,128)(2,1)S(1)}, bf16[2,8,1,4,32,512]{5,4,3,2,1,0:T(8,128)(2,1)}, u32[]{:S(2)}) copy-start(bf16[2,8,1,4,32,512]{5,4,3,2,1,0:T(8,128)(2,1)} %get-tuple-element.28) | copy-start | bytes 6291460
  117.4 53.4 %all-to-all-start.3 = ((bf16[8,2,4,32,512]{4,3,2,1,0:T(8,128)(2,1)}), bf16[8,2,4,32,512]{4,3,2,1,0:T(8,128)(2,1)}, u32[]{:S(2)}, u32[]{:S(2)}) async-start(bf16[8,2,4,32,512]{4,3,2,1,0:T(8,128)(2,1)} %get-tuple-element.22), calls=%async_computation.3 | async-start | bytes 4194304 | tf_op jit(solution)/shard_map/all_to_all | solution.py:380
  138.5 36.8 %copy-start = (bf16[48,256,128]{2,1,0:T(8,128)(2,1)S(1)}, bf16[48,256,128]{2,1,0:T(8,128)(2,1)}, u32[]{:S(2)}) copy-start(bf16[48,256,128]{2,1,0:T(8,128)(2,1)} %beams.6) | copy-start | bytes 9437188
  170.8 53.4 %all-to-all-start.1 = ((bf16[8,2,4,32,512]{4,3,2,1,0:T(8,128)(2,1)}), bf16[8,2,4,32,512]{4,3,2,1,0:T(8,128)(2,1)}, u32[]{:S(2)}, u32[]{:S(2)}) async-start(bf16[8,2,4,32,512]{4,3,2,1,0:T(8,128)(2,1)} %get-tuple-element.21), calls=%async_computation.1 | async-start | bytes 4194304 | tf_op jit(solution)/shard_map/all_to_all | solution.py:380
  175.4 4.6 %copy-start.1 = (bf16[48,256,128]{2,1,0:T(8,128)(2,1)S(1)}, bf16[48,256,128]{2,1,0:T(8,128)(2,1)}, u32[]{:S(2)}) copy-start(bf16[48,256,128]{2,1,0:T(8,128)(2,1)} %beams.4) | copy-start | bytes 9437188
  176.5 37.3 %collective-permute-start.10 = (bf16[12,256,128]{2,1,0:T(8,128)(2,1)S(1)}, bf16[12,256,128]{2,1,0:T(8,128)(2,1)S(1)}, u32[]{:S(2)}, u32[]{:S(2)}) collective-permute-start(bf16[12,256,128]{2,1,0:T(8,128)(2,1)S(1)} %get-tuple-element.30), channel_id=1, source_target_pairs={{0,16},{8,24},{16,0},{24,8},{1,17},{9,25},{17,1},{25,9},{2,18},{10... | collective-permute-start | bytes 2359304 | tf_op jit(solution)/shard_map/ppermute | solution.py:389
  178.0 38.2 %collective-permute-start.11 = (bf16[12,256,128]{2,1,0:T(8,128)(2,1)S(1)}, bf16[12,256,128]{2,1,0:T(8,128)(2,1)S(1)}, u32[]{:S(2)}, u32[]{:S(2)}) collective-permute-start(bf16[12,256,128]{2,1,0:T(8,128)(2,1)S(1)} %get-tuple-element.29), channel_id=1, source_target_pairs={{0,24},{8,16},{16,8},{24,0},{1,25},{9,17},{17,9},{25,1},{2,26},{10... | collective-permute-start | bytes 2359304 | tf_op jit(solution)/shard_map/ppermute | solution.py:389
  179.4 64.6 %collective-permute-start.9 = (bf16[12,256,128]{2,1,0:T(8,128)(2,1)}, bf16[12,256,128]{2,1,0:T(8,128)(2,1)S(1)}, u32[]{:S(2)}, u32[]{:S(2)}) collective-permute-start(bf16[12,256,128]{2,1,0:T(8,128)(2,1)} %get-tuple-element.31), channel_id=1, source_target_pairs={{0,8},{8,0},{16,24},{24,16},{1,9},{9,1},{17,25},{25,17},{2,10},{10... | collective-permute-start | bytes 2359304 | tf_op jit(solution)/shard_map/ppermute | solution.py:389
  181.5 64.0 %collective-permute-start.6 = (bf16[12,256,128]{2,1,0:T(8,128)(2,1)}, bf16[12,256,128]{2,1,0:T(8,128)(2,1)S(1)}, u32[]{:S(2)}, u32[]{:S(2)}) collective-permute-start(bf16[12,256,128]{2,1,0:T(8,128)(2,1)} %get-tuple-element.34), channel_id=1, source_target_pairs={{0,8},{8,0},{16,24},{24,16},{1,9},{9,1},{17,25},{25,17},{2,10},{10... | collective-permute-start | bytes 2359304 | tf_op jit(solution)/shard_map/ppermute | solution.py:389
  183.0 64.0 %collective-permute-start.7 = (bf16[12,256,128]{2,1,0:T(8,128)(2,1)}, bf16[12,256,128]{2,1,0:T(8,128)(2,1)}, u32[]{:S(2)}, u32[]{:S(2)}) collective-permute-start(bf16[12,256,128]{2,1,0:T(8,128)(2,1)} %get-tuple-element.33), channel_id=1, source_target_pairs={{0,16},{8,24},{16,0},{24,8},{1,17},{9,25},{17,1},{25,9},{2,18},{10... | collective-permute-start | bytes 2359304 | tf_op jit(solution)/shard_map/ppermute | solution.py:389
  213.7 27.2 %copy-start.5 = (bf16[12,256,128]{2,1,0:T(8,128)(2,1)}, bf16[12,256,128]{2,1,0:T(8,128)(2,1)S(1)}, u32[]{:S(2)}) copy-start(bf16[12,256,128]{2,1,0:T(8,128)(2,1)S(1)} %collective-permute-done.10.refs_6_) | copy-start | bytes 2359300
  213.7 36.2 %collective-permute-start.8 = (bf16[12,256,128]{2,1,0:T(8,128)(2,1)}, bf16[12,256,128]{2,1,0:T(8,128)(2,1)}, u32[]{:S(2)}, u32[]{:S(2)}) collective-permute-start(bf16[12,256,128]{2,1,0:T(8,128)(2,1)} %get-tuple-element.32), channel_id=1, source_target_pairs={{0,24},{8,16},{16,8},{24,0},{1,25},{9,17},{17,9},{25,1},{2,26},{10... | collective-permute-start | bytes 2359304 | tf_op jit(solution)/shard_map/ppermute | solution.py:389
  216.2 24.8 %copy-start.6 = (bf16[12,256,128]{2,1,0:T(8,128)(2,1)}, bf16[12,256,128]{2,1,0:T(8,128)(2,1)S(1)}, u32[]{:S(2)}) copy-start(bf16[12,256,128]{2,1,0:T(8,128)(2,1)S(1)} %collective-permute-done.11.refs_7_) | copy-start | bytes 2359300
  216.2 49.7 %collective-permute-start.3 = (bf16[12,256,128]{2,1,0:T(8,128)(2,1)}, bf16[12,256,128]{2,1,0:T(8,128)(2,1)}, u32[]{:S(2)}, u32[]{:S(2)}) collective-permute-start(bf16[12,256,128]{2,1,0:T(8,128)(2,1)} %get-tuple-element.37), channel_id=1, source_target_pairs={{0,8},{8,0},{16,24},{24,16},{1,9},{9,1},{17,25},{25,17},{2,10},{10... | collective-permute-start | bytes 2359304 | tf_op jit(solution)/shard_map/ppermute | solution.py:389
  244.0 24.3 %copy-start.7 = (bf16[12,256,128]{2,1,0:T(8,128)(2,1)}, bf16[12,256,128]{2,1,0:T(8,128)(2,1)S(1)}, u32[]{:S(2)}) copy-start(bf16[12,256,128]{2,1,0:T(8,128)(2,1)S(1)} %collective-permute-done.9.refs_5_) | copy-start | bytes 2359300
  244.0 36.1 %collective-permute-start.4 = (bf16[12,256,128]{2,1,0:T(8,128)(2,1)}, bf16[12,256,128]{2,1,0:T(8,128)(2,1)S(1)}, u32[]{:S(2)}, u32[]{:S(2)}) collective-permute-start(bf16[12,256,128]{2,1,0:T(8,128)(2,1)} %get-tuple-element.36), channel_id=1, source_target_pairs={{0,16},{8,24},{16,0},{24,8},{1,17},{9,25},{17,1},{25,9},{2,18},{10... | collective-permute-start | bytes 2359304 | tf_op jit(solution)/shard_map/ppermute | solution.py:389
  245.6 22.7 %copy-start.8 = (bf16[12,256,128]{2,1,0:T(8,128)(2,1)}, bf16[12,256,128]{2,1,0:T(8,128)(2,1)S(1)}, u32[]{:S(2)}) copy-start(bf16[12,256,128]{2,1,0:T(8,128)(2,1)S(1)} %collective-permute-done.6.refs_1_) | copy-start | bytes 2359300
  245.6 38.0 %collective-permute-start.5 = (bf16[12,256,128]{2,1,0:T(8,128)(2,1)}, bf16[12,256,128]{2,1,0:T(8,128)(2,1)S(1)}, u32[]{:S(2)}, u32[]{:S(2)}) collective-permute-start(bf16[12,256,128]{2,1,0:T(8,128)(2,1)} %get-tuple-element.35), channel_id=1, source_target_pairs={{0,24},{8,16},{16,8},{24,0},{1,25},{9,17},{17,9},{25,1},{2,26},{10... | collective-permute-start | bytes 2359304 | tf_op jit(solution)/shard_map/ppermute | solution.py:389
  247.0 52.6 %collective-permute-start = (bf16[12,256,128]{2,1,0:T(8,128)(2,1)}, bf16[12,256,128]{2,1,0:T(8,128)(2,1)}, u32[]{:S(2)}, u32[]{:S(2)}) collective-permute-start(bf16[12,256,128]{2,1,0:T(8,128)(2,1)} %get-tuple-element.40), channel_id=1, source_target_pairs={{0,8},{8,0},{16,24},{24,16},{1,9},{9,1},{17,25},{25,17},{2,10},{10... | collective-permute-start | bytes 2359304 | tf_op jit(solution)/shard_map/ppermute | solution.py:389
  249.9 50.5 %collective-permute-start.1 = (bf16[12,256,128]{2,1,0:T(8,128)(2,1)}, bf16[12,256,128]{2,1,0:T(8,128)(2,1)}, u32[]{:S(2)}, u32[]{:S(2)}) collective-permute-start(bf16[12,256,128]{2,1,0:T(8,128)(2,1)} %get-tuple-element.39), channel_id=1, source_target_pairs={{0,16},{8,24},{16,0},{24,8},{1,17},{9,25},{17,1},{25,9},{2,18},{10... | collective-permute-start | bytes 2359304 | tf_op jit(solution)/shard_map/ppermute | solution.py:389
  265.8 50.5 %collective-permute-start.2 = (bf16[12,256,128]{2,1,0:T(8,128)(2,1)}, bf16[12,256,128]{2,1,0:T(8,128)(2,1)}, u32[]{:S(2)}, u32[]{:S(2)}) collective-permute-start(bf16[12,256,128]{2,1,0:T(8,128)(2,1)} %get-tuple-element.38), channel_id=1, source_target_pairs={{0,24},{8,16},{16,8},{24,0},{1,25},{9,17},{17,9},{25,1},{2,26},{10... | collective-permute-start | bytes 2359304 | tf_op jit(solution)/shard_map/ppermute | solution.py:389
  280.1 36.3 %copy-start.9 = (bf16[12,256,128]{2,1,0:T(8,128)(2,1)}, bf16[12,256,128]{2,1,0:T(8,128)(2,1)S(1)}, u32[]{:S(2)}) copy-start(bf16[12,256,128]{2,1,0:T(8,128)(2,1)S(1)} %collective-permute-done.4.refs_6_) | copy-start | bytes 2359300
  283.6 32.8 %copy-start.10 = (bf16[12,256,128]{2,1,0:T(8,128)(2,1)}, bf16[12,256,128]{2,1,0:T(8,128)(2,1)S(1)}, u32[]{:S(2)}) copy-start(bf16[12,256,128]{2,1,0:T(8,128)(2,1)S(1)} %collective-permute-done.5.refs_7_) | copy-start | bytes 2359300
